TPU v7x, 512 devices: a whole 4x8x8 slice. The times are simulated.
512 devices in a mesh: shard: 64 (over x, z, core), rep: 8 (over y).
Axes of the slice: x: 4, y: 8, z: 8, core: 2. Of those that a mesh axis runs over, the one named last changes fastest.
Arguments:
- attn_grad: bfloat16 [8, 2, 4, 768, 768], P('rep', None, None, 'shard'), may hold values from -16 to 16
- attn_error: float32 [8, 2, 4, 768, 768], P('rep', None, None, 'shard'), may hold values from -6 to 6
- attn_basis: float32 [2, 4, 768, 32], P(None, None, 'shard'), may hold values from -0.21875 to 0.21875
- attn_roots: float32 [2, 4, 3, 32, 32], replicated, as said below
- attn_momentum: float32 [2, 4, 768, 768], P(None, None, 'shard'), may hold values from -4 to 4
- attn_weights: float32 [2, 4, 768, 768], P(None, None, 'shard'), may hold values from -0.21875 to 0.21875
- mlp_grad: bfloat16 [8, 2, 2, 768, 3072], P('rep', None, None, 'shard'), may hold values from -16 to 16
- mlp_error: float32 [8, 2, 2, 768, 3072], P('rep', None, None, 'shard'), may hold values from -6 to 6
- mlp_basis: float32 [2, 2, 3072, 32], P(None, None, 'shard'), may hold values from -0.109375 to 0.109375
- mlp_roots: float32 [2, 2, 3, 32, 32], replicated, as said below
- mlp_momentum: float32 [2, 2, 768, 3072], P(None, None, 'shard'), may hold values from -4 to 4
- mlp_weights: float32 [2, 2, 768, 3072], P(None, None, 'shard'), may hold values from -0.21875 to 0.21875
- small_grad: bfloat16 [8, 2, 9984], P('rep', None, 'shard'), may hold values from -6 to 6
- small_momentum: float32 [2, 9984], P(None, 'shard'), may hold values from -4 to 4
- small_weights: float32 [2, 9984], P(None, 'shard'), may hold values from -6 to 6
Outputs:
- attn_error_out: float32 [8, 2, 4, 768, 768], P('rep', None, None, 'shard')
- mlp_error_out: float32 [8, 2, 2, 768, 3072], P('rep', None, None, 'shard')
- attn_left: float32 [2, 4, 768, 32], P(None, None, 'shard')
- attn_right: float32 [2, 4, 768, 32], P(None, None, 'shard')
- mlp_left: float32 [2, 2, 768, 32], P(None, None, 'shard')
- mlp_right: float32 [2, 2, 3072, 32], P(None, None, 'shard')
- attn_momentum_out: float32 [2, 4, 768, 768], P(None, None, 'shard')
- attn_weights_out: float32 [2, 4, 768, 768], P(None, None, 'shard')
- mlp_momentum_out: float32 [2, 2, 768, 3072], P(None, None, 'shard')
- mlp_weights_out: float32 [2, 2, 768, 3072], P(None, None, 'shard')
- small_momentum_out: float32 [2, 9984], P(None, 'shard')
- small_weights_out: float32 [2, 9984], P(None, 'shard')
Inputs may be any that keep to these rules, and one draw needn't show every extreme that they name: Every 32 x 32 factor of attn_roots is a scaled identity plus independent entries and is well conditioned. Every 32 x 32 factor of mlp_roots is a scaled identity plus independent entries and is well conditioned.
All inputs are finite; a program needn't handle non-finite values.
Results may differ from a plain program's by a relative error of at most 0.0003.
Values sent between devices are 32-bit elements; how exact they have to be, the bound alone decides.
A program may use at most 64 MiB of HBM per device.

v0:
```python
import jax
import jax.numpy as jnp
from jax import lax
from jax.sharding import PartitionSpec as P

momentum_decay = 0.9
learn_rate = 0.05


def rows_product(merged, factor):
    return jnp.einsum("lkrc,lkcn->lkrn", merged, factor, precision=lax.Precision.HIGHEST)


def cols_product(merged, factor):
    return jnp.einsum("lkrc,lkrn->lkcn", merged, factor, precision=lax.Precision.HIGHEST)


def rotate(factor, inverse_roots, round_index):
    return jnp.einsum(
        "lkrn,lknm->lkrm", factor, inverse_roots[:, :, round_index], precision=lax.Precision.HIGHEST
    )


def finish(summed, inverse_roots, round_index):
    if round_index < 0:
        return summed / float(lax.axis_size("rep"))
    return rotate(summed, inverse_roots, round_index)


def own_share(full_factor):
    share_width = full_factor.shape[2] // lax.axis_size("shard")
    share_start = lax.axis_index("shard") * share_width
    return lax.dynamic_slice_in_dim(full_factor, share_start, share_width, 2)


def column_round(attn_term, mlp_term, attn_roots, mlp_roots, round_index):
    attn_full, mlp_full = lax.psum((attn_term, mlp_term), ("shard", "rep"))
    attn_full = finish(attn_full, attn_roots, round_index)
    mlp_full = finish(mlp_full, mlp_roots, round_index)
    attn_share = own_share(attn_full)
    mlp_share = own_share(mlp_full)
    attn_next, mlp_next = (attn_full, mlp_full)
    return (attn_next, mlp_next, attn_full, mlp_full, attn_share, mlp_share)


def update(merged, approx, momentum, weights):
    error_out = (merged - approx)[None]
    momentum_out = momentum_decay * momentum + approx
    weights_out = weights - learn_rate * momentum_out
    return (error_out, momentum_out, weights_out)


def per_device(
    attn_grad,
    attn_error,
    attn_basis,
    attn_roots,
    attn_momentum,
    attn_weights,
    mlp_grad,
    mlp_error,
    mlp_basis,
    mlp_roots,
    mlp_momentum,
    mlp_weights,
    small_grad,
    small_momentum,
    small_weights,
):
    attn_merged = attn_grad[0].astype(jnp.float32) + attn_error[0]
    mlp_merged = mlp_grad[0].astype(jnp.float32) + mlp_error[0]
    small_local = small_grad[0].astype(jnp.float32)
    attn_bfull, mlp_bfull = (
        lax.all_gather(attn_basis, "shard", axis=2, tiled=True),
        lax.all_gather(mlp_basis, "shard", axis=2, tiled=True),
    )
    attn_data, mlp_data = (attn_merged, mlp_merged)
    attn_start, mlp_start = (attn_bfull, mlp_bfull)
    attn_first = rows_product(attn_data, attn_start)
    mlp_first = rows_product(mlp_data, mlp_start)
    small_total = lax.psum(small_local, "rep")
    attn_first, mlp_first = lax.psum((attn_first, mlp_first), "rep")
    attn_lhat = rotate(attn_first, attn_roots, 0)
    mlp_lhat = rotate(mlp_first, mlp_roots, 0)
    attn_rhat, mlp_rhat, spare_one, spare_two, spare_three, spare_four = column_round(
        cols_product(attn_data, attn_lhat),
        cols_product(mlp_data, mlp_lhat),
        attn_roots,
        mlp_roots,
        1,
    )
    attn_second, mlp_second = lax.psum(
        (rows_product(attn_data, attn_rhat), rows_product(mlp_data, mlp_rhat)), "rep"
    )
    attn_left = rotate(attn_second, attn_roots, 2)
    mlp_left = rotate(mlp_second, mlp_roots, 2)
    spare_five, spare_six, attn_rfull, mlp_rfull, attn_right, mlp_right = column_round(
        cols_product(attn_data, attn_left),
        cols_product(mlp_data, mlp_left),
        attn_roots,
        mlp_roots,
        -1,
    )
    attn_approx = jnp.einsum(
        "lkrn,lkcn->lkrc", attn_left, attn_rfull, precision=lax.Precision.HIGHEST
    )
    mlp_approx = jnp.einsum("lkrn,lkcn->lkrc", mlp_left, mlp_rfull, precision=lax.Precision.HIGHEST)
    attn_error_out, attn_momentum_out, attn_weights_out = update(
        attn_merged, attn_approx, attn_momentum, attn_weights
    )
    mlp_error_out, mlp_momentum_out, mlp_weights_out = update(
        mlp_merged, mlp_approx, mlp_momentum, mlp_weights
    )
    small_mean = small_total / float(lax.axis_size("rep"))
    small_momentum_out = momentum_decay * small_momentum + small_mean
    small_weights_out = small_weights - learn_rate * small_momentum_out
    return (
        attn_error_out,
        mlp_error_out,
        attn_left,
        attn_right,
        mlp_left,
        mlp_right,
        attn_momentum_out,
        attn_weights_out,
        mlp_momentum_out,
        mlp_weights_out,
        small_momentum_out,
        small_weights_out,
    )


def solution(mesh):
    in_specs = (
        P("rep", None, None, "shard", None),
        P("rep", None, None, "shard", None),
        P(None, None, "shard", None),
        P(),
        P(None, None, "shard", None),
        P(None, None, "shard", None),
        P("rep", None, None, "shard", None),
        P("rep", None, None, "shard", None),
        P(None, None, "shard", None),
        P(),
        P(None, None, "shard", None),
        P(None, None, "shard", None),
        P("rep", None, "shard"),
        P(None, "shard"),
        P(None, "shard"),
    )
    out_specs = (
        P("rep", None, None, "shard", None),
        P("rep", None, None, "shard", None),
        P(None, None, "shard", None),
        P(None, None, "shard", None),
        P(None, None, "shard", None),
        P(None, None, "shard", None),
        P(None, None, "shard", None),
        P(None, None, "shard", None),
        P(None, None, "shard", None),
        P(None, None, "shard", None),
        P(None, "shard"),
        P(None, "shard"),
    )
    return jax.shard_map(
        per_device, mesh=mesh, in_specs=in_specs, out_specs=out_specs, check_vma=False
    )
```

profile of v0, /device:TPU:1, one launch (start us, length us, event | category | flops | bytes accessed | tf_op | source)
XLA Modules:
  0.0 757.0 jit_solution(16800400785792100691)
XLA Ops:
  7.2 0.0 all-gather.2.cloned.1.call-start
  7.2 1.6 copy.101
  8.8 0.0 all-gather.2.cloned.1.call-update
  8.8 0.0 all-reduce.9.cloned.1.call-start
  8.9 0.8 copy.94
  9.7 0.0 copy-start.2
  9.7 0.0 copy-start.3
  9.7 59.7 %all_gather.6 = f32[2,4,768,32]{3,1,0,2:T(4,128)S(1)} all-gather(f32[2,4,12,32]{3,1,0,2:T(4,128)S(1)} %copy.94), channel_id=1, replica_groups=mesh['shard'=64,'rep'=8] {'shard'}, dimensions={2}, use_global_device_ids=true | all-gather | bytes 798720 | tf_op jit(solution)/shard_map/all_gather | solution.py:74
  69.4 0.0 copy-done.2
  69.4 0.0 copy-done.3
  69.4 0.0 copy-start
  69.4 0.0 copy-start.1
  69.4 2.1 fusion.2
  71.5 0.0 copy-start.11
  71.6 33.6 %all-gather.2.cloned.1.call-done = f32[2,2,3072,32]{3,1,0,2:T(2,128)} async-done(((f32[2,2,48,32]{3,1,0,2:T(2,128)}), f32[2,2,3072,32]{3,1,0,2:T(2,128)}) %all-gather.2.cloned.1.call-update) | async-done | bytes 1572880 | tf_op jit(solution)/shard_map/all_gather | solution.py:75
  105.2 0.0 copy-done
  105.2 0.0 copy-done.1
  105.2 6.1 fusion
  111.3 0.0 copy-start.12
  111.3 23.7 %all-reduce.3 = (f32[2,4,12,32]{3,2,1,0:T(8,128)S(1)}, f32[2,2,12,32]{3,2,1,0:T(8,128)S(1)}) all-reduce(f32[2,4,12,32]{3,2,1,0:T(8,128)S(1)} %fusion.2, f32[2,2,12,32]{3,2,1,0:T(8,128)S(1)} %fusion), channel_id=1, replica_groups=mesh['shard'=64,'rep'=8] {'rep'}, use_global_device_ids=true, to_apply=%region_0.0 | all-reduce | flops 4608 | bytes 36864 | tf_op jit(solution)/shard_map/psum | solution.py:82
  135.1 0.0 copy-done.11
  135.1 0.2 fusion.26
  135.3 1.7 fusion.17
  137.0 0.0 copy-done.12
  137.0 0.2 fusion.35
  137.2 2.8 fusion.8
  140.0 0.0 all-reduce.9.cloned.1.call-update
  140.0 0.2 all-reduce.7.cloned.1.call-start
  140.3 0.4 copy-done.15
  140.7 279.9 %all-reduce.9.cloned.1.call-done = (f32[2,4,768,32]{2,3,1,0:T(8,128)}, f32[2,2,3072,32]{2,3,1,0:T(8,128)}) async-done(((f32[2,4,768,32]{2,3,1,0:T(8,128)}, f32[2,2,3072,32]{2,3,1,0:T(8,128)}), (f32[2,4,768,32]{2,3,1,0:T(8,128)}, f32[2,2,3072,32]{2,3,1,0:T(8,128)})) %all-reduce.9.cloned.1.call-update) | async-done | bytes 2359312 | tf_op jit(solution)/shard_map/psum | solution.py:37
  420.6 2.1 fusion.22
  422.7 0.8 fusion.15
  423.5 1.5 fusion.31
  424.9 1.6 fusion.6
  426.6 23.4 %all-reduce.2 = (f32[2,4,12,32]{3,2,1,0:T(8,128)S(1)}, f32[2,2,12,32]{3,2,1,0:T(8,128)S(1)}, f32[2,156]{1,0:T(2,128)S(1)}) all-reduce(f32[2,4,12,32]{3,2,1,0:T(8,128)S(1)} %fusion.15, f32[2,2,12,32]{3,2,1,0:T(8,128)S(1)} %fusion.6, f32[2,156]{1,0:T(2,128)S(1)} %bitcast_convert_fusion), channel_id=1, replica_groups=mesh['shard'=64,'rep'=8] {'rep'}, use_global_device_ids=true, to_apply=%region_2.0 | all-reduce | flops 4920 | bytes 39360 | tf_op jit(solution)/shard_map/psum | solution.py:92
  450.0 0.2 fusion.24
  450.2 0.2 fusion.33
  450.4 1.7 fusion.13
  452.1 2.8 fusion.4
  454.9 0.0 all-reduce.7.cloned.1.call-update
  454.9 0.0 copy-start.9
  454.9 0.0 copy-start.10
  454.9 0.6 copy.114
  455.6 0.6 copy.112
  456.2 0.0 copy-done.14
  456.2 0.6 multiply_subtract_fusion
  456.8 280.8 %all-reduce.7.cloned.1.call-done = (f32[2,4,768,32]{2,3,1,0:T(8,128)}, f32[2,2,3072,32]{2,3,1,0:T(8,128)}) async-done(((f32[2,4,768,32]{2,3,1,0:T(8,128)}, f32[2,2,3072,32]{2,3,1,0:T(8,128)}), (f32[2,4,768,32]{2,3,1,0:T(8,128)}, f32[2,2,3072,32]{2,3,1,0:T(8,128)})) %all-reduce.7.cloned.1.call-update) | async-done | bytes 2359312 | tf_op jit(solution)/shard_map/psum | solution.py:37
  737.6 1.3 broadcast_multiply_fusion.1
  738.9 0.1 constant_dynamic-slice_fusion.1
  739.0 0.7 copy.113
  739.7 0.0 copy-done.9
  739.7 0.0 copy-done.5
  739.7 0.7 copy_subtract_fusion.1
  740.4 0.9 copy.116
  741.3 0.9 copy.115
  742.2 0.9 copy.110
  743.1 0.1 broadcast_multiply_fusion
  743.3 0.9 copy-done.7
  744.2 0.2 copy-done.8
  744.4 1.5 copy_subtract_fusion
  745.9 1.3 copy.118
  747.2 1.3 copy.117
  748.5 1.3 copy.111
  749.7 0.7 constant_dynamic-slice_fusion
  (13 shorter events, 0.0 us)
Async XLA Ops:
  7.2 98.0 %all-gather.2.cloned.1.call-start = ((), (), s32[]{:S(2)}) async-start(), calls=%async_computation | async-start | bytes 6389760 | tf_op jit(solution)/shard_map/all_gather | solution.py:75
  8.8 411.8 %all-reduce.9.cloned.1.call-start = ((), (), s32[]{:S(2)}) async-start(), calls=%async_computation.2 | async-start | bytes 4718592 | tf_op jit(solution)/shard_map/psum | solution.py:37
  9.7 59.7 %copy-start.2 = (f32[1,2,4,12,768]{4,2,3,1,0:T(4,128)S(1)}, f32[1,2,4,12,768]{4,2,3,1,0:T(4,128)}, u32[]{:S(2)}) copy-start(f32[1,2,4,12,768]{4,2,3,1,0:T(4,128)} %param.16) | copy-start | bytes 884740
  9.7 59.7 %copy-start.3 = (bf16[1,2,4,12,768]{4,2,3,1,0:T(4,128)(2,1)S(1)}, bf16[1,2,4,12,768]{4,2,3,1,0:T(4,128)(2,1)}, u32[]{:S(2)}) copy-start(bf16[1,2,4,12,768]{4,2,3,1,0:T(4,128)(2,1)} %param.15) | copy-start | bytes 442372
  69.4 35.8 %copy-start = (f32[1,2,2,12,3072]{4,2,3,1,0:T(2,128)S(1)}, f32[1,2,2,12,3072]{4,2,3,1,0:T(2,128)}, u32[]{:S(2)}) copy-start(f32[1,2,2,12,3072]{4,2,3,1,0:T(2,128)} %param.22) | copy-start | bytes 1769476
  69.4 35.8 %copy-start.1 = (bf16[1,2,2,12,3072]{4,2,3,1,0:T(2,128)(2,1)S(1)}, bf16[1,2,2,12,3072]{4,2,3,1,0:T(2,128)(2,1)}, u32[]{:S(2)}) copy-start(bf16[1,2,2,12,3072]{4,2,3,1,0:T(2,128)(2,1)} %param.21) | copy-start | bytes 884740
  71.5 63.5 %copy-start.11 = (f32[2,4,3,32,32]{4,3,2,1,0:T(8,128)S(1)}, f32[2,4,3,32,32]{4,3,2,1,0:T(8,128)}, u32[]{:S(2)}) copy-start(f32[2,4,3,32,32]{4,3,2,1,0:T(8,128)} %param.18) | copy-start | bytes 294916
  111.3 25.7 %copy-start.12 = (f32[2,2,3,32,32]{4,3,2,1,0:T(8,128)S(1)}, f32[2,2,3,32,32]{4,3,2,1,0:T(8,128)}, u32[]{:S(2)}) copy-start(f32[2,2,3,32,32]{4,3,2,1,0:T(8,128)} %param.24) | copy-start | bytes 147460
  140.0 0.7 copy-start.15
  140.0 597.6 %all-reduce.7.cloned.1.call-start = ((), (), s32[]{:S(2)}) async-start(), calls=%async_computation.1 | async-start | bytes 4718592 | tf_op jit(solution)/shard_map/psum | solution.py:37
  420.6 2.9 copy-start.6
  454.9 1.3 copy-start.13
  454.9 1.3 copy-start.14
  454.9 284.8 %copy-start.9 = (f32[2,4,12,768]{3,1,2,0:T(4,128)S(1)}, f32[2,4,12,768]{3,1,2,0:T(4,128)}, u32[]{:S(2)}) copy-start(f32[2,4,12,768]{3,1,2,0:T(4,128)} %param.20) | copy-start | bytes 884740
  454.9 284.8 %copy-start.10 = (f32[2,4,12,768]{3,1,2,0:T(4,128)S(1)}, f32[2,4,12,768]{3,1,2,0:T(4,128)}, u32[]{:S(2)}) copy-start(f32[2,4,12,768]{3,1,2,0:T(4,128)} %param.19) | copy-start | bytes 884740
  737.6 2.1 copy-start.5
  740.4 2.7 copy-start.4
  743.1 1.1 copy-start.7
  743.1 1.2 copy-start.8
Sparse Core Ops, SparseCore 0:
  11.9 93.1 all-gather.1
  140.1 280.3 all-reduce.8
  455.0 282.5 all-reduce.6
where the time goes:
time: 757 us
  waiting for transfers between devices  594 us (78%)
  blocking collectives  107 us (14%)
  matrix products  26.2 us (3%)
  between operations  14 us (2%)
  local copies, waits for them, and re-layouts  13.3 us (2%)
    psum x2, waiting for transfers between devices, column_round(): attn_full, mlp_full = lax.psum((attn_term, mlp_term), ('shard', 'rep'))  561 us
    all_gather x1, blocking collectives, per_device(): lax.all_gather(attn_basis, 'shard', axis=2, tiled=True)  59.7 us
    all_gather x1, waiting for transfers between devices, per_device(): lax.all_gather(mlp_basis, 'shard', axis=2, tiled=True)  33.6 us
    psum x1, blocking collectives, per_device(): attn_first, mlp_first = lax.psum((attn_first, mlp_first), 'rep')  23.7 us
    psum x1, blocking collectives, per_device(): lax.psum((rows_product(attn_data, attn_rhat), rows_product(mlp_data, mlp_...  23.4 us
  transfers between devices with their start and end apart: 3, of which 3 were waited for; matrix products, arithmetic and copies ran while one was open for 1% of the time, Pallas kernels for 0%

commit v1 on v0

--- a/solution.py
+++ b/solution.py
@@ -34,7 +34,7 @@
 
 
 def column_round(attn_term, mlp_term, attn_roots, mlp_roots, round_index):
-    attn_full, mlp_full = lax.psum((attn_term, mlp_term), ("shard", "rep"))
+    attn_full, mlp_full = lax.psum(lax.psum((attn_term, mlp_term), "shard"), "rep")
     attn_full = finish(attn_full, attn_roots, round_index)
     mlp_full = finish(mlp_full, mlp_roots, round_index)
     attn_share = own_share(attn_full)

time: 757 us -> 784 us (1.036)
  waiting for transfers between devices: 594 us -> 618 us
    psum x2 -> x4, waiting for transfers between devices: 561 us -> 585 us  [the longest x2 410 us: column_round(): lax.psum((attn_term, mlp_term), 'shard')]
  transfers between devices with their start and end apart: 3 -> 5, of which waited for: 3 -> 5; matrix products, arithmetic and copies ran while one was open for 1% -> 1% of each run, Pallas kernels for 0% -> 0%
where the time goes in v1:
time: 784 us; the launch traced here: 781 us
  waiting for transfers between devices  618 us (79%)
  blocking collectives  107 us (14%)
  matrix products  26.2 us (3%)
  between operations  14 us (2%)
  local copies, waits for them, and re-layouts  12.9 us (2%)
    psum x2, waiting for transfers between devices, column_round(): lax.psum((attn_term, mlp_term), 'shard')  410 us
    psum x2, waiting for transfers between devices, column_round(): lax.psum(lax.psum((attn_term, mlp_term), 'shard'), 'rep')  174 us
    all_gather x1, blocking collectives, per_device(): lax.all_gather(attn_basis, 'shard', axis=2, tiled=True)  59.7 us
    all_gather x1, waiting for transfers between devices, per_device(): lax.all_gather(mlp_basis, 'shard', axis=2, tiled=True)  33.6 us
    psum x1, blocking collectives, per_device(): attn_first, mlp_first = lax.psum((attn_first, mlp_first), 'rep')  23.7 us
    psum x1, blocking collectives, per_device(): lax.psum((rows_product(attn_data, attn_rhat), rows_product(mlp_data, mlp_...  23.6 us
  transfers between devices with their start and end apart: 5, of which 5 were waited for; matrix products, arithmetic and copies ran while one was open for 1% of the time, Pallas kernels for 0%

profile of v1, /device:TPU:1, one launch (start us, length us, event | category | flops | bytes accessed | tf_op | source)
XLA Modules:
  0.0 781.0 jit_solution(3708317513811696136)
XLA Ops:
  7.2 0.0 all-gather.2.cloned.1.call-start
  7.2 1.6 copy.101
  8.8 0.0 all-gather.2.cloned.1.call-update
  8.8 0.0 all-reduce.13.cloned.1.call-start
  8.9 0.8 copy.94
  9.7 0.0 copy-start.2
  9.7 0.0 copy-start.3
  9.7 59.7 %all_gather.6 = f32[2,4,768,32]{3,1,0,2:T(4,128)S(1)} all-gather(f32[2,4,12,32]{3,1,0,2:T(4,128)S(1)} %copy.94), channel_id=1, replica_groups=mesh['shard'=64,'rep'=8] {'shard'}, dimensions={2}, use_global_device_ids=true | all-gather | bytes 798720 | tf_op jit(solution)/shard_map/all_gather | solution.py:74
  69.4 0.0 copy-start
  69.4 0.0 copy-start.1
  69.4 2.1 fusion.2
  71.5 0.0 copy-start.11
  71.6 33.6 %all-gather.2.cloned.1.call-done = f32[2,2,3072,32]{3,1,0,2:T(2,128)} async-done(((f32[2,2,48,32]{3,1,0,2:T(2,128)}), f32[2,2,3072,32]{3,1,0,2:T(2,128)}) %all-gather.2.cloned.1.call-update) | async-done | bytes 1572880 | tf_op jit(solution)/shard_map/all_gather | solution.py:75
  105.2 6.1 fusion
  111.3 0.0 copy-start.12
  111.3 23.7 %all-reduce.3 = (f32[2,4,12,32]{3,2,1,0:T(8,128)S(1)}, f32[2,2,12,32]{3,2,1,0:T(8,128)S(1)}) all-reduce(f32[2,4,12,32]{3,2,1,0:T(8,128)S(1)} %fusion.2, f32[2,2,12,32]{3,2,1,0:T(8,128)S(1)} %fusion), channel_id=1, replica_groups=mesh['shard'=64,'rep'=8] {'rep'}, use_global_device_ids=true, to_apply=%region_0.0 | all-reduce | flops 4608 | bytes 36864 | tf_op jit(solution)/shard_map/psum | solution.py:82
  135.1 0.0 copy-done.11
  135.1 0.2 fusion.26
  135.3 1.7 fusion.17
  137.0 0.2 fusion.35
  137.2 2.8 fusion.8
  140.0 0.0 all-reduce.13.cloned.1.call-update
  140.0 0.0 copy-start.15
  140.0 0.0 all-reduce.17.cloned.1.call-start
  140.1 201.0 %all-reduce.13.cloned.1.call-done = (f32[2,4,768,32]{2,3,1,0:T(8,128)}, f32[2,2,3072,32]{2,3,1,0:T(8,128)}) async-done(((f32[2,4,768,32]{2,3,1,0:T(8,128)}, f32[2,2,3072,32]{2,3,1,0:T(8,128)}), (f32[2,4,768,32]{2,3,1,0:T(8,128)}, f32[2,2,3072,32]{2,3,1,0:T(8,128)})) %all-reduce.13.cloned.1.call-update) | async-done | bytes 2359312 | tf_op jit(solution)/shard_map/psum | solution.py:37
  341.0 0.0 all-reduce.17.cloned.1.call-update
  341.1 0.2 all-reduce.11.cloned.1.call-start
  341.3 88.0 %all-reduce.17.cloned.1.call-done = (f32[2,4,768,32]{2,3,1,0:T(8,128)}, f32[2,2,3072,32]{2,3,1,0:T(8,128)}) async-done(((f32[2,4,768,32]{2,3,1,0:T(8,128)}, f32[2,2,3072,32]{2,3,1,0:T(8,128)}), (f32[2,4,768,32]{2,3,1,0:T(8,128)}, f32[2,2,3072,32]{2,3,1,0:T(8,128)})) %all-reduce.17.cloned.1.call-update) | async-done | bytes 2359312 | tf_op jit(solution)/shard_map/psum | solution.py:37
  429.3 2.1 fusion.22
  431.4 0.8 fusion.15
  432.2 1.5 fusion.31
  433.7 1.6 fusion.6
  435.3 23.6 %all-reduce.2 = (f32[2,4,12,32]{3,2,1,0:T(8,128)S(1)}, f32[2,2,12,32]{3,2,1,0:T(8,128)S(1)}, f32[2,156]{1,0:T(2,128)S(1)}) all-reduce(f32[2,4,12,32]{3,2,1,0:T(8,128)S(1)} %fusion.15, f32[2,2,12,32]{3,2,1,0:T(8,128)S(1)} %fusion.6, f32[2,156]{1,0:T(2,128)S(1)} %bitcast_convert_fusion), channel_id=1, replica_groups=mesh['shard'=64,'rep'=8] {'rep'}, use_global_device_ids=true, to_apply=%region_3.0 | all-reduce | flops 4920 | bytes 39360 | tf_op jit(solution)/shard_map/psum | solution.py:92
  458.9 0.2 fusion.24
  459.2 0.2 fusion.33
  459.4 1.7 fusion.13
  461.1 2.8 fusion.4
  463.9 0.0 all-reduce.11.cloned.1.call-update
  463.9 0.0 copy-start.13
  463.9 0.0 copy-start.14
  463.9 0.3 all-reduce.15.cloned.1.call-start
  464.2 209.3 %all-reduce.11.cloned.1.call-done = (f32[2,4,768,32]{2,3,1,0:T(8,128)}, f32[2,2,3072,32]{2,3,1,0:T(8,128)}) async-done(((f32[2,4,768,32]{2,3,1,0:T(8,128)}, f32[2,2,3072,32]{2,3,1,0:T(8,128)}), (f32[2,4,768,32]{2,3,1,0:T(8,128)}, f32[2,2,3072,32]{2,3,1,0:T(8,128)})) %all-reduce.11.cloned.1.call-update) | async-done | bytes 2359312 | tf_op jit(solution)/shard_map/psum | solution.py:37
  673.5 0.0 all-reduce.15.cloned.1.call-update
  673.5 0.0 copy-start.9
  673.6 0.0 copy-start.10
  673.6 0.6 copy.114
  674.2 0.6 copy.112
  674.8 0.6 multiply_subtract_fusion
  675.4 86.2 %all-reduce.15.cloned.1.call-done = (f32[2,4,768,32]{2,3,1,0:T(8,128)}, f32[2,2,3072,32]{2,3,1,0:T(8,128)}) async-done(((f32[2,4,768,32]{2,3,1,0:T(8,128)}, f32[2,2,3072,32]{2,3,1,0:T(8,128)}), (f32[2,4,768,32]{2,3,1,0:T(8,128)}, f32[2,2,3072,32]{2,3,1,0:T(8,128)})) %all-reduce.15.cloned.1.call-update) | async-done | bytes 2359312 | tf_op jit(solution)/shard_map/psum | solution.py:37
  761.7 1.3 broadcast_multiply_fusion.1
  762.9 0.1 constant_dynamic-slice_fusion.1
  763.0 0.7 copy.113
  763.8 0.7 copy_subtract_fusion.1
  764.5 0.9 copy.116
  765.4 0.9 copy.115
  766.3 0.9 copy.110
  767.2 0.1 broadcast_multiply_fusion
  767.4 0.9 copy-done.7
  768.3 0.2 copy-done.8
  768.4 1.5 copy_subtract_fusion
  770.0 1.3 copy.118
  771.3 1.3 copy.117
  772.5 1.3 copy.111
  773.8 0.7 constant_dynamic-slice_fusion
  (19 shorter events, 0.0 us)
Async XLA Ops:
  7.2 98.0 %all-gather.2.cloned.1.call-start = ((), (), s32[]{:S(2)}) async-start(), calls=%async_computation | async-start | bytes 6389760 | tf_op jit(solution)/shard_map/all_gather | solution.py:75
  8.8 332.2 %all-reduce.13.cloned.1.call-start = ((), (), s32[]{:S(2)}) async-start(), calls=%async_computation.2 | async-start | bytes 4718592 | tf_op jit(solution)/shard_map/psum | solution.py:37
  9.7 59.7 %copy-start.2 = (f32[1,2,4,12,768]{4,2,3,1,0:T(4,128)S(1)}, f32[1,2,4,12,768]{4,2,3,1,0:T(4,128)}, u32[]{:S(2)}) copy-start(f32[1,2,4,12,768]{4,2,3,1,0:T(4,128)} %param.16) | copy-start | bytes 884740
  9.7 59.7 %copy-start.3 = (bf16[1,2,4,12,768]{4,2,3,1,0:T(4,128)(2,1)S(1)}, bf16[1,2,4,12,768]{4,2,3,1,0:T(4,128)(2,1)}, u32[]{:S(2)}) copy-start(bf16[1,2,4,12,768]{4,2,3,1,0:T(4,128)(2,1)} %param.15) | copy-start | bytes 442372
  69.4 35.8 %copy-start = (f32[1,2,2,12,3072]{4,2,3,1,0:T(2,128)S(1)}, f32[1,2,2,12,3072]{4,2,3,1,0:T(2,128)}, u32[]{:S(2)}) copy-start(f32[1,2,2,12,3072]{4,2,3,1,0:T(2,128)} %param.22) | copy-start | bytes 1769476
  69.4 35.8 %copy-start.1 = (bf16[1,2,2,12,3072]{4,2,3,1,0:T(2,128)(2,1)S(1)}, bf16[1,2,2,12,3072]{4,2,3,1,0:T(2,128)(2,1)}, u32[]{:S(2)}) copy-start(bf16[1,2,2,12,3072]{4,2,3,1,0:T(2,128)(2,1)} %param.21) | copy-start | bytes 884740
  71.5 63.5 %copy-start.11 = (f32[2,4,3,32,32]{4,3,2,1,0:T(8,128)S(1)}, f32[2,4,3,32,32]{4,3,2,1,0:T(8,128)}, u32[]{:S(2)}) copy-start(f32[2,4,3,32,32]{4,3,2,1,0:T(8,128)} %param.18) | copy-start | bytes 294916
  111.3 25.7 %copy-start.12 = (f32[2,2,3,32,32]{4,3,2,1,0:T(8,128)S(1)}, f32[2,2,3,32,32]{4,3,2,1,0:T(8,128)}, u32[]{:S(2)}) copy-start(f32[2,2,3,32,32]{4,3,2,1,0:T(8,128)} %param.24) | copy-start | bytes 147460
  140.0 201.3 %copy-start.15 = (bf16[1,2,156]{2,1,0:T(2,128)(2,1)S(1)}, bf16[1,2,156]{2,1,0:T(2,128)(2,1)}, u32[]{:S(2)}) copy-start(bf16[1,2,156]{2,1,0:T(2,128)(2,1)} %param.27) | copy-start | bytes 1876
  140.0 289.3 %all-reduce.17.cloned.1.call-start = ((), (), s32[]{:S(2)}) async-start(), calls=%async_computation.4 | async-start | bytes 4718592 | tf_op jit(solution)/shard_map/psum | solution.py:37
  341.1 332.5 %all-reduce.11.cloned.1.call-start = ((), (), s32[]{:S(2)}) async-start(), calls=%async_computation.1 | async-start | bytes 4718592 | tf_op jit(solution)/shard_map/psum | solution.py:37
  429.3 2.9 copy-start.6
  463.9 211.0 %copy-start.13 = (f32[2,156]{1,0:T(2,128)S(1)}, f32[2,156]{1,0:T(2,128)}, u32[]{:S(2)}) copy-start(f32[2,156]{1,0:T(2,128)} %param.29) | copy-start | bytes 3748
  463.9 211.0 %copy-start.14 = (f32[2,156]{1,0:T(2,128)S(1)}, f32[2,156]{1,0:T(2,128)}, u32[]{:S(2)}) copy-start(f32[2,156]{1,0:T(2,128)} %param.28) | copy-start | bytes 3748
  463.9 297.8 %all-reduce.15.cloned.1.call-start = ((), (), s32[]{:S(2)}) async-start(), calls=%async_computation.3 | async-start | bytes 4718592 | tf_op jit(solution)/shard_map/psum | solution.py:37
  673.5 90.2 %copy-start.9 = (f32[2,4,12,768]{3,1,2,0:T(4,128)S(1)}, f32[2,4,12,768]{3,1,2,0:T(4,128)}, u32[]{:S(2)}) copy-start(f32[2,4,12,768]{3,1,2,0:T(4,128)} %param.20) | copy-start | bytes 884740
  673.6 90.2 %copy-start.10 = (f32[2,4,12,768]{3,1,2,0:T(4,128)S(1)}, f32[2,4,12,768]{3,1,2,0:T(4,128)}, u32[]{:S(2)}) copy-start(f32[2,4,12,768]{3,1,2,0:T(4,128)} %param.19) | copy-start | bytes 884740
  761.7 2.1 copy-start.5
  764.5 2.7 copy-start.4
  767.2 1.1 copy-start.7
  767.2 1.2 copy-start.8
Sparse Core Ops, SparseCore 0:
  11.9 93.1 all-gather.1
  140.1 200.8 all-reduce.12
  343.5 85.8 all-reduce.16
  464.0 209.4 all-reduce.10
  675.8 85.8 all-reduce.14
